TPU v7x, 128 devices: a whole 4x4x4 slice. The times are simulated.
128 devices in a mesh: sec: 2 (over z_lo), row: 8 (over x, z_hi), col: 8 (over y, core).
Axes of the slice: x: 4, y: 4, z: 4 (z_hi: 2, z_lo: 2; z = z_hi * 2 + z_lo), core: 2. Of those that a mesh axis runs over, the one named last changes fastest.
Arguments:
- held_inverse: bfloat16 [12288, 12288], P('row', ('sec', 'col')), as said below
- factor_panels: bfloat16 [2, 12288, 1024], P(None, ('sec', 'col'), 'row'), may hold values from -0.125 to 0.125
- block_inverses: bfloat16 [2, 1024, 1024], P(None, 'row'), as said below
- covariance: float32 [12288, 12288], P('row', ('sec', 'col')), may hold values from -0.9 to 0.9
Outputs:
- updated: float32 [12288, 12288], P('row', ('sec', 'col'))
Inputs may be any that keep to these rules, and one draw needn't show every extreme that they name: held_inverse is lower triangular with a positive diagonal. Each block of block_inverses is lower triangular with a positive diagonal.
All inputs are finite; a program needn't handle non-finite values.
Results may differ from a plain program's by a relative error of at most 0.0038.
Values may be sent and summed in bfloat16 or wider, within the bound.
A program may use at most 128 MiB of HBM per device.

v0:
```python
import jax
import jax.numpy as jnp
from jax import lax
from jax.sharding import Mesh
from jax.sharding import PartitionSpec as P

PANELS = 2
ROW = ("row_0", "row_1")


def scatter_axes(x, axes, dim):
    for axis in axes:
        x = lax.psum_scatter(x, axis, scatter_dimension=dim, tiled=True)
    return x


def from_root(x, axis, root):
    mine = lax.axis_index(axis) == root
    return lax.psum(jnp.where(mine, x, jnp.zeros_like(x)), axis)


def body(held_inverse, factor_panels, block_inverses, covariance):
    total = covariance
    tile_cols = held_inverse.shape[1]
    groups = lax.axis_size(("sec", "col"))
    ratio = groups // lax.axis_size(ROW)
    column_index = lax.axis_index(("sec", "col"))
    root_row = column_index // ratio
    offset = column_index % ratio * tile_cols
    for panel in range(PANELS):
        partial_value = jnp.dot(
            factor_panels[panel], block_inverses[panel], preferred_element_type=jnp.float32
        )
        scaled = scatter_axes(partial_value, ROW, 1).astype(jnp.bfloat16)
        terms = jnp.dot(
            held_inverse,
            lax.all_gather(scaled, ROW, axis=1, tiled=True),
            preferred_element_type=jnp.float32,
        )
        summed = lax.psum(terms, ("sec", "col"))
        inverse = (-summed).astype(jnp.bfloat16)
        own_block = lax.dynamic_slice_in_dim(inverse, offset, tile_cols, 0)
        column_block = from_root(own_block, ROW, root_row)
        total = total + lax.dot_general(
            inverse, column_block, (((1,), (1,)), ((), ())), preferred_element_type=jnp.float32
        )
    return total


def solution(mesh):
    split = Mesh(
        mesh.devices.reshape(mesh.shape["sec"], 4, 2, mesh.shape["col"]),
        ("sec", "row_0", "row_1", "col"),
    )
    in_specs = (
        P(ROW, ("sec", "col")),
        P(None, ("sec", "col"), ROW),
        P(None, ROW, None),
        P(ROW, ("sec", "col")),
    )
    out_specs = P(ROW, ("sec", "col"))
    return jax.shard_map(body, mesh=split, in_specs=in_specs, out_specs=out_specs, check_vma=False)
```

profile of v0, /device:TPU:1, one launch (start us, length us, event | category | flops | bytes accessed | tf_op | source)
XLA Modules:
  0.0 582.4 jit_solution(17937898365134801965)
XLA Ops:
  6.5 0.0 copy-start
  6.5 0.0 copy-start.4
  6.5 0.0 copy-start.5
  6.5 0.0 reduce-scatter.5.cloned.1.call-start
  6.5 3.4 fusion.2
  10.0 0.0 reduce-scatter.5.cloned.1.call-update
  10.0 0.0 reduce-scatter.9.cloned.1.call-start
  10.0 0.0 copy-done.4
  10.0 0.0 copy-done.5
  10.1 2.2 fusion
  12.3 0.0 reduce-scatter.9.cloned.1.call-update
  12.3 0.0 reduce-scatter.7.cloned.1.call-start
  12.3 39.2 %reduce-scatter.5.cloned.1.call-done = f32[768,256]{1,0:T(8,128)} async-done(((f32[768,1024]{1,0:T(8,128)}), f32[768,256]{1,0:T(8,128)}) %reduce-scatter.5.cloned.1.call-update) | async-done | bytes 786448 | tf_op jit(solution)/shard_map/reduce_scatter | solution.py:13
  51.5 0.0 reduce-scatter.7.cloned.1.call-update
  51.6 0.0 reduce-scatter.11.cloned.1.call-start
  51.6 40.3 %reduce-scatter.9.cloned.1.call-done = f32[768,256]{1,0:T(8,128)} async-done(((f32[768,1024]{1,0:T(8,128)}), f32[768,256]{1,0:T(8,128)}) %reduce-scatter.9.cloned.1.call-update) | async-done | bytes 786448 | tf_op jit(solution)/shard_map/reduce_scatter | solution.py:13
  91.9 0.0 reduce-scatter.11.cloned.1.call-update
  92.0 0.0 all-gather.3.cloned.1.call-start
  92.0 23.7 %reduce-scatter.7.cloned.1.call-done = f32[768,128]{1,0:T(8,128)} async-done(((f32[768,256]{1,0:T(8,128)}), f32[768,128]{1,0:T(8,128)}) %reduce-scatter.7.cloned.1.call-update) | async-done | bytes 393232 | tf_op jit(solution)/shard_map/reduce_scatter | solution.py:13
  115.7 1.7 convert_element_type.12
  117.4 0.0 all-gather.3.cloned.1.call-update
  117.4 0.0 all-gather.5.cloned.1.call-start
  117.4 21.4 %reduce-scatter.11.cloned.1.call-done = f32[768,128]{1,0:T(8,128)} async-done(((f32[768,256]{1,0:T(8,128)}), f32[768,128]{1,0:T(8,128)}) %reduce-scatter.11.cloned.1.call-update) | async-done | bytes 393232 | tf_op jit(solution)/shard_map/reduce_scatter | solution.py:13
  138.8 1.7 convert_element_type.14
  140.5 0.0 all-gather.5.cloned.1.call-update
  140.6 0.0 all-reduce.5.cloned.1.call-start
  140.6 50.5 %all-gather.3.cloned.1.call-done = bf16[768,1024]{1,0:T(8,128)(2,1)} async-done(((bf16[768,128]{1,0:T(8,128)(2,1)}), bf16[768,1024]{1,0:T(8,128)(2,1)}) %all-gather.3.cloned.1.call-update) | async-done | bytes 1572880 | tf_op jit(solution)/shard_map/all_gather | solution.py:37
  191.1 0.0 copy-done
  191.1 6.1 %convolution_bitcast_fusion.1 = f32[1536,1024]{0,1:T(8,128)} fusion(bf16[768,1024]{1,0:T(8,128)(2,1)} %all-gather.3.cloned.1.call-done, bf16[1536,768]{1,0:T(8,128)(2,1)S(1)} %copy-done), kind=kOutput, calls=%fused_computation.4 | convolution fusion | flops 2415919104 | bytes 10223616 | tf_op jit(solution)/shard_map/dot_general | solution.py:35
  197.2 47.0 %all-gather.5.cloned.1.call-done = bf16[768,1024]{1,0:T(8,128)(2,1)} async-done(((bf16[768,128]{1,0:T(8,128)(2,1)}), bf16[768,1024]{1,0:T(8,128)(2,1)}) %all-gather.5.cloned.1.call-update) | async-done | bytes 1572880 | tf_op jit(solution)/shard_map/all_gather | solution.py:37
  244.2 6.0 %convolution_bitcast_fusion = f32[1536,1024]{0,1:T(8,128)} fusion(bf16[768,1024]{1,0:T(8,128)(2,1)} %all-gather.5.cloned.1.call-done, bf16[1536,768]{1,0:T(8,128)(2,1)S(1)} %copy-done), kind=kOutput, calls=%fused_computation.3 | convolution fusion | flops 2415919104 | bytes 10223616 | tf_op jit(solution)/shard_map/dot_general | solution.py:35
  250.1 0.0 all-reduce.5.cloned.1.call-update
  250.2 0.0 all-reduce.7.cloned.1.call-start
  250.3 158.0 %all-reduce.5.cloned.1.call-done = (f32[1536,1024]{0,1:T(8,128)}, f32[1536,1024]{0,1:T(8,128)}) async-done(((f32[1536,1024]{0,1:T(8,128)}, f32[1536,1024]{0,1:T(8,128)}), (f32[1536,1024]{0,1:T(8,128)}, f32[1536,1024]{0,1:T(8,128)})) %all-reduce.5.cloned.1.call-update) | async-done | bytes 12582928 | tf_op jit(solution)/shard_map/psum | solution.py:40
  408.2 6.3 %negate_convert_fusion = (bf16[1536,1024]{0,1:T(8,128)(2,1)S(1)}, bf16[1536,1024]{0,1:T(8,128)(2,1)S(1)}) fusion(f32[1536,1024]{0,1:T(8,128)} %get-tuple-element.6, f32[1536,1024]{0,1:T(8,128)} %get-tuple-element.5), kind=kLoop, calls=%fused_computation | loop fusion | flops 6291456 | bytes 18874368 | tf_op jit(solution)/shard_map/convert_element_type | solution.py:41
  414.5 0.0 copy-start.2
  414.6 1.7 dynamic-slice_select_fusion.1
  416.3 0.4 copy-done.2
  416.7 1.5 dynamic-slice_select_fusion
  418.2 0.0 all-reduce.7.cloned.1.call-update
  418.3 146.6 %all-reduce.7.cloned.1.call-done = (bf16[768,1024]{0,1:T(8,128)(2,1)}, bf16[768,1024]{0,1:T(8,128)(2,1)}) async-done(((bf16[768,1024]{0,1:T(8,128)(2,1)}, bf16[768,1024]{0,1:T(8,128)(2,1)}), (bf16[768,1024]{0,1:T(8,128)(2,1)}, bf16[768,1024]{0,1:T(8,128)(2,1)})) %all-reduce.7.cloned.1.call-update) | async-done | bytes 3145744 | tf_op jit(solution)/shard_map/psum | solution.py:19
  564.9 0.0 copy-start.3
  564.9 0.0 copy-start.6
  564.9 4.3 fusion.10
  569.2 0.0 copy-done.3
  569.2 0.0 copy-done.6
  569.2 0.0 copy-start.1
  569.2 6.4 %add_add_fusion = f32[1536,768]{1,0:T(8,128)} fusion(f32[1536,768]{1,0:T(8,128)} %param.7, f32[1536,768]{1,0:T(8,128)S(1)} %fusion.10, bf16[1536,1024]{0,1:T(8,128)(2,1)S(1)} %copy-done.3, bf16[768,1024]{0,1:T(8,128)(2,1)S(1)} %copy-done.6), kind=kOutput, calls=%fused_computation.2 | convolution fusion | flops 2418278400 | bytes 18874368 | tf_op jit(solution)/shard_map/dot_general | solution.py:44
  575.6 0.0 copy-done.1
Async XLA Ops:
  6.5 184.6 %copy-start = (bf16[1536,768]{1,0:T(8,128)(2,1)S(1)}, bf16[1536,768]{1,0:T(8,128)(2,1)}, u32[]{:S(2)}) copy-start(bf16[1536,768]{1,0:T(8,128)(2,1)} %param.4) | copy-start | bytes 7077892
  6.5 3.5 copy-start.4
  6.5 3.5 copy-start.5
  6.5 45.0 %reduce-scatter.5.cloned.1.call-start = ((), (), s32[]{:S(2)}) async-start(), calls=%async_computation.4 | async-start | bytes 3932160 | tf_op jit(solution)/shard_map/reduce_scatter | solution.py:13
  10.0 82.0 %reduce-scatter.9.cloned.1.call-start = ((), (), s32[]{:S(2)}) async-start(), calls=%async_computation.7 | async-start | bytes 3932160 | tf_op jit(solution)/shard_map/reduce_scatter | solution.py:13
  12.3 103.4 %reduce-scatter.7.cloned.1.call-start = ((), (), s32[]{:S(2)}) async-start(), calls=%async_computation.5 | async-start | bytes 1179648 | tf_op jit(solution)/shard_map/reduce_scatter | solution.py:13
  51.6 87.3 %reduce-scatter.11.cloned.1.call-start = ((), (), s32[]{:S(2)}) async-start(), calls=%async_computation.8 | async-start | bytes 1179648 | tf_op jit(solution)/shard_map/reduce_scatter | solution.py:13
  92.0 99.1 %all-gather.3.cloned.1.call-start = ((), (), s32[]{:S(2)}) async-start(), calls=%async_computation.6 | async-start | bytes 1769472 | tf_op jit(solution)/shard_map/all_gather | solution.py:37
  117.4 126.8 %all-gather.5.cloned.1.call-start = ((), (), s32[]{:S(2)}) async-start(), calls=%async_computation.9 | async-start | bytes 1769472 | tf_op jit(solution)/shard_map/all_gather | solution.py:37
  140.6 267.7 %all-reduce.5.cloned.1.call-start = ((), (), s32[]{:S(2)}) async-start(), calls=%async_computation.10 | async-start | bytes 25165824 | tf_op jit(solution)/shard_map/psum | solution.py:40
  250.2 314.7 %all-reduce.7.cloned.1.call-start = ((), (), s32[]{:S(2)}) async-start(), calls=%async_computation.11 | async-start | bytes 6291456 | tf_op jit(solution)/shard_map/psum | solution.py:19
  414.5 2.2 copy-start.2
  564.9 4.3 copy-start.3
  564.9 4.4 copy-start.6
  569.2 6.4 %copy-start.1 = (bf16[1536,768]{1,0:T(8,128)(2,1)S(1)}, bf16[1536,768]{1,0:T(8,128)(2,1)}, u32[]{:S(2)}) copy-start(bf16[1536,768]{1,0:T(8,128)(2,1)} %param.4) | copy-start | bytes 7077892
Sparse Core Ops, SparseCore 0:
  10.1 41.3 reduce-scatter.4
  53.9 37.9 reduce-scatter.8
  94.3 21.3 reduce-scatter.6
  117.9 20.8 reduce-scatter.10
  140.9 50.1 all-gather.2
  193.1 51.0 all-gather.4
  250.3 157.9 all-reduce.4
  418.4 146.4 all-reduce.6
where the time goes:
time: 586 us; the launch traced here: 582 us
  waiting for transfers between devices  527 us (90%)
  matrix products  28.4 us (5%)
  between operations  13.6 us (2%)
  other arithmetic  12.9 us (2%)
    psum x1, waiting for transfers between devices, body(): summed = lax.psum(terms, ('sec', 'col'))  158 us
    psum x1, waiting for transfers between devices, from_root(): return lax.psum(jnp.where(mine, x, jnp.zeros_like(x)), axis)  147 us
    reduce_scatter x4, waiting for transfers between devices, scatter_axes(): x = lax.psum_scatter(x, axis, scatter_dimension=dim, tiled=True)  125 us
    all_gather x2, waiting for transfers between devices, body(): lax.all_gather(scaled, ROW, axis=1, tiled=True)  97.4 us
    dot_general x2, matrix products, body(): jnp.dot(held_inverse, lax.all_gather(scaled, ROW, axis=1, tiled=True), pr...  12.1 us
  transfers between devices with their start and end apart: 8, of which 8 were waited for; matrix products, arithmetic and copies ran while one was open for 2% of the time, Pallas kernels for 0%

commit v1 on v0

v1 whole, which is shorter than its diff:
```python
import jax
import jax.numpy as jnp
from jax import lax
from jax.experimental import pallas as pl
from jax.experimental.pallas import tpu as pltpu
from jax.sharding import Mesh
from jax.sharding import PartitionSpec as P

MESH = pl.DeviceIdType.MESH
AXES = ("zl", "x", "zh", "y", "k")
BF16 = jnp.bfloat16
F32 = jnp.float32

CHUNKS = 4
SPREAD = 3


def al(i, n):
    return pl.multiple_of(i, n)


def kernel(
    l_ref, f_ref, d_ref, c_ref, out_ref,
    lb, g, db, s, t, own, rs1, rs2, rsz, ir, iq, cb, send, recv, local,
):
    zl, x, zh, y, k = (lax.axis_index(a) for a in AXES)
    rows, cols = l_ref.shape
    _, _, fcols = f_ref.shape
    drows, width = d_ref.shape[1:]
    wide = width // CHUNKS
    part = rows // 8
    pair = 2 * part
    r = 2 * x + zh
    xp, xm = lax.rem(x + 1, 4), lax.rem(x + 3, 4)
    yp, ym, y2 = lax.rem(y + 1, 4), lax.rem(y + 3, 4), lax.rem(y + 2, 4)
    piece = 2 * y + zl

    ys, zs = 2 * lax.rem(x, 2) + zh, x // 2
    d_to, e_to = lax.rem(y - ys + 4, 4), lax.rem(zl + zs, 2)
    tr_to = {"zl": zs, "x": lax.rem(x + d_to, 4), "zh": lax.rem(zh + e_to, 2), "y": ys}
    xs, hs = 2 * zl + y // 2, lax.rem(y, 2)
    d_from, e_from = lax.rem(x - xs + 4, 4), lax.rem(zh + hs, 2)
    tr_from = {"zl": lax.rem(zl + e_from, 2), "x": xs, "zh": hs, "y": lax.rem(y + d_from, 4)}
    diagonal = jnp.logical_and(d_to == 0, e_to == 0)
    got = 2 * lax.rem(y + d_from, 4) + lax.rem(zl + e_from, 2)
    gotz = 2 * lax.rem(y + d_from, 4) + lax.rem(zl + e_from + 1, 2)
    bx = lax.rem(y + d_from, 4)
    bxp, bxm = lax.rem(bx + 1, 4), lax.rem(bx + 3, 4)

    group = [
        {"x": lax.rem(x + dx, 4), "zh": lax.rem(zh + dz, 2)}
        for dx in range(4) for dz in range(2) if dx or dz
    ]
    peers = group + [
        {"k": 1 - k}, {"zh": 1 - zh, "k": 1 - k}, {"x": xp, "k": 1 - k}, {"x": xm, "k": 1 - k},
        {"zl": 1 - zl}, {"y": yp}, {"y": ym},
    ]
    barrier = pltpu.get_barrier_semaphore()
    for peer in peers:
        pl.semaphore_signal(barrier, inc=1, device_id=peer, device_id_type=MESH)

    @pl.when(jnp.logical_not(diagonal))
    def _():
        pl.semaphore_signal(barrier, inc=1, device_id=tr_to, device_id_type=MESH)
        pl.semaphore_signal(barrier, inc=1, device_id=tr_from, device_id_type=MESH)
        pl.semaphore_wait(barrier, len(peers) + 2)

    @pl.when(diagonal)
    def _():
        pl.semaphore_wait(barrier, len(peers))

    counts = {"remote": 0, "local": 0}
    sent = []

    def remote(src, dst, device):
        n = counts["remote"]
        counts["remote"] += 1
        copy = pltpu.make_async_remote_copy(
            src_ref=src, dst_ref=dst, send_sem=send.at[n], recv_sem=recv.at[n],
            device_id=device, device_id_type=MESH,
        )
        sent.append(copy)
        copy.start()
        return copy

    def here(src, dst):
        n = counts["local"]
        counts["local"] += 1
        copy = pltpu.make_async_copy(src, dst, local.at[n])
        copy.start()
        return copy

    def at_f(xx, kk, hh):
        return g.at[xx, pl.ds(al(kk * cols, cols), cols), pl.ds(al(hh * fcols, fcols), fcols)]

    mine = f_ref.at[k]
    other = f_ref.at[1 - k]
    slot = at_f(x, k, zh)
    f_own = here(mine, slot)
    f_z = [remote(mine, slot, {"zh": 1 - zh}), remote(other, slot, {"zh": 1 - zh, "k": 1 - k})]
    f_k = remote(other, slot, {"k": 1 - k})
    f_x = [
        remote(mine, slot, {"x": xp}), remote(other, slot, {"x": xp, "k": 1 - k}),
        remote(mine, slot, {"x": xm}), remote(other, slot, {"x": xm, "k": 1 - k}),
    ]
    dpart = drows // 8
    dsrc = d_ref.at[k, pl.ds(al(piece * dpart, dpart), dpart), :]
    d_own = here(dsrc, db.at[r, piece])
    d_r = [remote(dsrc, db.at[r, piece], peer) for peer in group]
    l_own = here(l_ref, lb.at[k])
    l_k = remote(l_ref, lb.at[k], {"k": 1 - k})
    c_own = here(c_ref, cb)

    d_own.wait()
    for copy in d_r:
        copy.wait_recv()
    d_z = remote(db.at[:, piece], db.at[:, piece], {"zl": 1 - zl})
    for copy in f_z:
        copy.wait_recv()
    ahead = g.at[x, :, pl.ds(al((1 - zh) * fcols, fcols), fcols)]
    f_x2 = [remote(ahead, ahead, {"x": xp}), remote(ahead, ahead, {"x": xm})]
    d_z.wait_recv()
    two = db.at[:, pl.ds(2 * y, 2)]
    d_y = [remote(two, two, {"y": yp}), remote(two, two, {"y": ym})]
    for copy in f_x + f_x2:
        copy.wait_recv()
    low, high = g.at[xm, pl.ds(0, cols)], g.at[xp, pl.ds(cols, cols)]
    f_x3 = [remote(low, low, {"x": xp}), remote(high, high, {"x": xm})]
    for copy in d_y:
        copy.wait_recv()
    low, high = db.at[:, 2 * ym], db.at[:, 2 * yp + 1]
    d_y2 = [remote(low, low, {"y": yp}), remote(high, high, {"y": ym})]
    f_own.wait()
    f_k.wait_recv()
    l_own.wait()
    l_k.wait_recv()
    for copy in d_y2 + f_x3:
        copy.wait_recv()

    block = 512
    steps = rows // block
    done = {}

    def slab(b):
        return pl.ds(al(b * pair, pair), pair)

    def thin(p):
        return pl.ds(al(p * part, part), part)

    def s1(c):
        lanes = slice(c * wide, (c + 1) * wide)
        first = c * wide // (2 * drows)

        @pl.loop(0, steps)
        def _(i):
            m = pl.ds(al(i * block, block), block)
            acc = None
            for xx in range(first, 4):
                rhs = db[2 * xx : 2 * xx + 2, :, :, lanes].reshape(2 * drows, wide)
                term = jnp.dot(g[xx, m, :], rhs, preferred_element_type=F32)
                acc = term if acc is None else acc + term
            s[m, :] = acc.astype(BF16)

        @pl.loop(0, steps)
        def _(i):
            m = pl.ds(al(i * block, block), block)
            acc = jnp.dot(lb[0, m, :], s[:cols, :], preferred_element_type=F32)
            acc += jnp.dot(lb[1, m, :], s[cols:, :], preferred_element_type=F32)
            t[c, m, :] = acc.astype(BF16)

        done["rs1", c] = [
            remote(t.at[c, thin(2 * y2)], rs1.at[c, 0], {"y": yp}),
            remote(t.at[c, thin(2 * y2 + 1)], rs1.at[c, 1], {"y": ym}),
        ]

    def s2(c):
        up, down = done["rs1", c]
        up.wait_recv()
        t[c, thin(2 * yp), :] = (t[c, thin(2 * yp), :].astype(F32) + rs1[c, 0].astype(F32)).astype(BF16)
        down.wait_recv()
        t[c, thin(2 * ym + 1), :] = (t[c, thin(2 * ym + 1), :].astype(F32) + rs1[c, 1].astype(F32)).astype(BF16)
        done["rs2", c] = [
            remote(t.at[c, slab(yp)], rs2.at[c, 0], {"y": yp}),
            remote(t.at[c, slab(ym)], rs2.at[c, 1], {"y": ym}),
        ]

    def s3(c):
        for copy in done["rs2", c]:
            copy.wait_recv()
        away = 1 - zl
        for dst, z in ((rsz.at[c, 0], away), (own.at[c], zl)):
            total = t[c, thin(2 * y + z), :].astype(F32)
            for side in range(2):
                total += rs2[c, side, pl.ds(al(z * part, part), part), :].astype(F32)
            dst[...] = total.astype(dst.dtype)
        done["rsz", c] = remote(rsz.at[c, 0], rsz.at[c, 1], {"zl": 1 - zl})

    def s4(c):
        done["rsz", c].wait_recv()
        ir[k, c, thin(piece), :] = (-(own[c] + rsz[c, 1].astype(F32))).astype(BF16)
        src = ir.at[k, c, thin(piece)]
        done["agz", c] = remote(src, src, {"zl": 1 - zl})
        n = counts["remote"]
        counts["remote"] += 1
        dst = iq.at[k, c, thin(piece)]
        away = pltpu.make_async_remote_copy(
            src_ref=src, dst_ref=dst, send_sem=send.at[n], recv_sem=recv.at[n], device_id=tr_to, device_id_type=MESH
        )
        still = pltpu.make_async_copy(src, dst, recv.at[n])
        done["tr", c] = away, still

        @pl.when(jnp.logical_not(diagonal))
        def _():
            away.start()

        @pl.when(diagonal)
        def _():
            still.start()

    def s5(c):
        done["agz", c].wait_recv()
        src = ir.at[k, c, slab(y)]
        done["agy", c] = [remote(src, src, {"y": yp}), remote(src, src, {"y": ym})]
        away, still = done["tr", c]

        @pl.when(jnp.logical_not(diagonal))
        def _():
            away.wait_recv()

        @pl.when(diagonal)
        def _():
            still.wait()

        src = iq.at[k, c, thin(got)]
        done["cgz", c] = remote(src, src, {"zh": 1 - zh})

    def s6(c):
        for copy in done["agy", c]:
            copy.wait_recv()
        low, high = ir.at[k, c, thin(2 * ym)], ir.at[k, c, thin(2 * yp + 1)]
        done["agy2", c] = [remote(low, low, {"y": yp}), remote(high, high, {"y": ym})]
        done["cgz", c].wait_recv()
        src = iq.at[k, c, slab(bx)]
        done["cgx", c] = [remote(src, src, {"x": xp}), remote(src, src, {"x": xm})]

    def s7(c):
        for copy in done["agy2", c]:
            copy.wait_recv()
        done["ir", c] = remote(ir.at[k, c], ir.at[k, c], {"k": 1 - k})
        for copy in done["cgx", c]:
            copy.wait_recv()
        low, high = iq.at[k, c, thin(2 * bxm)], iq.at[k, c, thin(2 * bxp + 1)]
        done["cgx2", c] = [remote(low, low, {"x": xp}), remote(high, high, {"x": xm})]

    def s8(c):
        for copy in done["cgx2", c]:
            copy.wait_recv()
        src = iq.at[k, c, pl.ds(al((1 - k) * cols, cols), cols)]
        done["iq", c] = remote(src, src, {"k": 1 - k})

    def s9(c):
        done["ir", c].wait_recv()
        done["iq", c].wait_recv()

        @pl.loop(0, steps)
        def _(i):
            m = pl.ds(al(i * block, block), block)
            acc = cb[m, :]
            for p in range(2):
                acc += lax.dot_general(
                    ir[p, c, m, :], iq[p, c, pl.ds(al(k * cols, cols), cols), :],
                    (((1,), (1,)), ((), ())), preferred_element_type=F32,
                )
            cb[m, :] = acc

    c_own.wait()
    stages = [s1, s2, s3, s4, s5, s6, s7, s8, s9]
    order = sorted(
        (turn * SPREAD + n, n, CHUNKS - 1 - turn) for turn in range(CHUNKS) for n in range(len(stages))
    )
    for _, n, c in order:
        stages[n](c)
    result = here(cb, out_ref)
    for copy in sent:
        copy.wait_send()
    for c in range(CHUNKS):
        @pl.when(jnp.logical_not(diagonal))
        def _():
            done["tr", c][0].wait_send()
    result.wait()


def solution(mesh):
    devices = mesh.devices
    split = Mesh(devices.reshape(2, 4, 2, 4, 2), AXES)

    def body(held, factor, inverses, covariance):
        rows, cols = held.shape
        fcols = factor.shape[2]
        drows, width = inverses.shape[1:]
        wide = width // CHUNKS
        part = rows // 8
        n_remote = 19 + 2 + 1 + 2 + 2 + 2 + 19 * CHUNKS
        return pl.pallas_call(
            kernel,
            out_shape=jax.ShapeDtypeStruct(covariance.shape, covariance.dtype),
            in_specs=[pl.BlockSpec(memory_space=pl.ANY)] * 4,
            out_specs=pl.BlockSpec(memory_space=pl.ANY),
            scratch_shapes=[
                pltpu.VMEM((2, rows, cols), BF16),
                pltpu.VMEM((4, 2 * cols, 2 * fcols), BF16),
                pltpu.VMEM((8, 8, drows // 8, width), BF16),
                pltpu.VMEM((2 * cols, wide), BF16),
                pltpu.VMEM((CHUNKS, rows, wide), BF16),
                pltpu.VMEM((CHUNKS, part, wide), F32),
                pltpu.VMEM((CHUNKS, 2, part, wide), BF16),
                pltpu.VMEM((CHUNKS, 2, 2 * part, wide), BF16),
                pltpu.VMEM((CHUNKS, 2, part, wide), BF16),
                pltpu.VMEM((2, CHUNKS, rows, wide), BF16),
                pltpu.VMEM((2, CHUNKS, rows, wide), BF16),
                pltpu.VMEM((rows, cols), F32),
                pltpu.SemaphoreType.DMA((n_remote,)),
                pltpu.SemaphoreType.DMA((n_remote,)),
                pltpu.SemaphoreType.DMA((8,)),
            ],
            compiler_params=pltpu.CompilerParams(
                collective_id=0, has_side_effects=True, vmem_limit_bytes=60 * 1024 * 1024
            ),
        )(held, factor, inverses, covariance)

    spec = P(("x", "zh"), ("zl", "y", "k"))
    return jax.shard_map(
        body,
        mesh=split,
        in_specs=(spec, P(None, ("zl", "y", "k"), ("x", "zh")), P(None, ("x", "zh"), None), spec),
        out_specs=spec,
        check_vma=False,
    )
```

time: 586 us -> 150 us (0.26)
  waiting for transfers between devices: 527 us -> 0 us
  Pallas kernels: 0 us -> 145 us
  matrix products: 28.4 us -> 0 us
  between operations: 13.6 us -> 0.01 us
  other arithmetic: 12.9 us -> 0 us
    psum x2 -> x0, waiting for transfers between devices: 305 us -> none  [the longest x1 158 us: body(): summed = lax.psum(terms, ('sec', 'col'))]
    pallas_call x0 -> x1, Pallas kernels: none -> 145 us  [body(): pl.pallas_call(kernel, out_shape=jax.ShapeDtypeStruct(covariance.shape, c...]
    reduce_scatter x4 -> x0, waiting for transfers between devices: 125 us -> none  [scatter_axes(): x = lax.psum_scatter(x, axis, scatter_dimension=dim, tiled=True)]
    all_gather x2 -> x0, waiting for transfers between devices: 97.4 us -> none  [body(): lax.all_gather(scaled, ROW, axis=1, tiled=True)]
    dot_general x6 -> x0, matrix products: 28.4 us -> none  [the longest x2 12.1 us: body(): jnp.dot(held_inverse, lax.all_gather(scaled, ROW, axis=1, tiled=True), pr...]
    convert_element_type x3 -> x0, other arithmetic: 9.69 us -> none  [the longest x1 6.29 us: body(): inverse = (-summed).astype(jnp.bfloat16)]
  transfers between devices with their start and end apart: 8 -> 0, of which waited for: 8 -> 0; matrix products, arithmetic and copies ran while one was open for 2% -> 0% of each run, Pallas kernels for 0% -> 0%
where the time goes in v1:
time: 150 us
  Pallas kernels  145 us (97%)
  local copies, waits for them, and re-layouts  4.83 us (3%)
    pallas_call x1, Pallas kernels, body(): pl.pallas_call(kernel, out_shape=jax.ShapeDtypeStruct(covariance.shape, c...  145 us
    unnamed x1, local copies, waits for them, and re-layouts  4.83 us

profile of v1, /device:TPU:1, one launch (start us, length us, event | category | flops | bytes accessed | tf_op | source)
XLA Modules:
  0.0 150.2 jit_solution(2616070897140785125)
XLA Ops:
  0.0 145.3 %shard_map.46 = f32[1536,768]{1,0:T(8,128)} custom-call(bf16[1536,768]{1,0:T(8,128)(2,1)} %l_ref.1, bf16[2,768,128]{2,1,0:T(8,128)(2,1)} %f_ref.1, bf16[2,128,1024]{2,1,0:T(8,128)(2,1)} %d_ref.1, f32[1536,768]{1,0:T(8,128)} %c_ref.1), custom_call_target="tpu_custom_call" | custom-call | tf_op jit(solution)/shard_map/pallas_call | solution.py:304
  145.3 4.8 %copy.6 = f32[1536,768]{1,0:T(8,128)} copy(f32[1536,768]{1,0:T(8,128)} %shard_map.46) | data formatting | bytes 9437184

commit v2 on v1

--- a/solution.py
+++ b/solution.py
@@ -12,7 +12,9 @@
 F32 = jnp.float32
 
 CHUNKS = 4
-SPREAD = 3
+SUB = 2
+START, PERIOD = 20.0, 2.7
+TIMES = (0.0, 2.8, 5.6, 8.4, 11.2, 13.9, 16.6, 19.3, 22.0)
 
 
 def al(i, n):
@@ -21,7 +23,7 @@
 
 def kernel(
     l_ref, f_ref, d_ref, c_ref, out_ref,
-    lb, g, db, s, t, own, rs1, rs2, rsz, ir, iq, cb, send, recv, local,
+    lb, g, db, s, t, own, rs1, rs2, rsz, ir, iq, cb, send, recv, send_f, recv_f, send_a, local,
 ):
     zl, x, zh, y, k = (lax.axis_index(a) for a in AXES)
     rows, cols = l_ref.shape
@@ -90,56 +92,114 @@
         copy.start()
         return copy
 
-    def at_f(xx, kk, hh):
-        return g.at[xx, pl.ds(al(kk * cols, cols), cols), pl.ds(al(hh * fcols, fcols), fcols)]
-
-    mine = f_ref.at[k]
-    other = f_ref.at[1 - k]
-    slot = at_f(x, k, zh)
-    f_own = here(mine, slot)
-    f_z = [remote(mine, slot, {"zh": 1 - zh}), remote(other, slot, {"zh": 1 - zh, "k": 1 - k})]
-    f_k = remote(other, slot, {"k": 1 - k})
-    f_x = [
-        remote(mine, slot, {"x": xp}), remote(other, slot, {"x": xp, "k": 1 - k}),
-        remote(mine, slot, {"x": xm}), remote(other, slot, {"x": xm, "k": 1 - k}),
-    ]
     dpart = drows // 8
     dsrc = d_ref.at[k, pl.ds(al(piece * dpart, dpart), dpart), :]
     d_own = here(dsrc, db.at[r, piece])
     d_r = [remote(dsrc, db.at[r, piece], peer) for peer in group]
+
+    sub = cols // SUB
+
+    def rows_f(h, u):
+        return pl.ds(al(h * cols + u * sub, sub), sub)
+
+    def lanes_f(hh):
+        return pl.ds(al(hh * fcols, fcols), fcols)
+
+    def src_f(p, u):
+        return f_ref.at[p, pl.ds(u * sub, sub), :]
+
+    slots = [g.at[x, rows_f(k, u), lanes_f(zh)] for u in range(SUB)]
+    f_z = [
+        [
+            remote(src_f(k, u), slots[u], {"zh": 1 - zh}),
+            remote(src_f(1 - k, u), slots[u], {"zh": 1 - zh, "k": 1 - k}),
+        ]
+        for u in range(SUB)
+    ]
+
+    def hop(c, h, ab, u):
+        n = ((c * 2 + h) * 2 + ab) * SUB + u
+        ref = g.at[c, rows_f(h, u), lanes_f(1 - zh if ab else zh)]
+        return pltpu.make_async_remote_copy(
+            src_ref=ref, dst_ref=ref, send_sem=send_f.at[n], recv_sem=recv_f.at[n],
+            device_id={"x": xm if h else xp}, device_id_type=MESH,
+        )
+
+    ahead = jnp.where(k == 0, xp, xm)
+    f_a = []
+    for u in range(SUB):
+        n = (x * 2 + k) * 2 * SUB + u
+        for p, device in ((k, {"x": ahead}), (1 - k, {"x": ahead, "k": 1 - k})):
+            copy = pltpu.make_async_remote_copy(
+                src_ref=src_f(p, u), dst_ref=slots[u], send_sem=send_a.at[len(f_a)], recv_sem=recv_f.at[n],
+                device_id=device, device_id_type=MESH,
+            )
+            copy.start()
+            f_a.append(copy)
+    own_slot = g.at[x, pl.ds(al(k * cols, cols), cols), lanes_f(zh)]
+    f_own = here(f_ref.at[k], own_slot)
+    f_k = remote(f_ref.at[1 - k], own_slot, {"k": 1 - k})
     l_own = here(l_ref, lb.at[k])
     l_k = remote(l_ref, lb.at[k], {"k": 1 - k})
     c_own = here(c_ref, cb)
-
-    d_own.wait()
-    for copy in d_r:
-        copy.wait_recv()
-    d_z = remote(db.at[:, piece], db.at[:, piece], {"zl": 1 - zl})
-    for copy in f_z:
-        copy.wait_recv()
-    ahead = g.at[x, :, pl.ds(al((1 - zh) * fcols, fcols), fcols)]
-    f_x2 = [remote(ahead, ahead, {"x": xp}), remote(ahead, ahead, {"x": xm})]
-    d_z.wait_recv()
-    two = db.at[:, pl.ds(2 * y, 2)]
-    d_y = [remote(two, two, {"y": yp}), remote(two, two, {"y": ym})]
-    for copy in f_x + f_x2:
-        copy.wait_recv()
-    low, high = g.at[xm, pl.ds(0, cols)], g.at[xp, pl.ds(cols, cols)]
-    f_x3 = [remote(low, low, {"x": xp}), remote(high, high, {"x": xm})]
-    for copy in d_y:
-        copy.wait_recv()
-    low, high = db.at[:, 2 * ym], db.at[:, 2 * yp + 1]
-    d_y2 = [remote(low, low, {"y": yp}), remote(high, high, {"y": ym})]
-    f_own.wait()
-    f_k.wait_recv()
-    l_own.wait()
-    l_k.wait_recv()
-    for copy in d_y2 + f_x3:
-        copy.wait_recv()
+    done = {}
+    moved = []
+
+    def when_at(c, n):
+        return lax.rem(x - c + 4, 4) == n
+
+    def relay(c, ab, u, n):
+        for h in range(2):
+            if n == 0 and ab == 0:
+                continue
+            @pl.when(when_at(c, (4 - n) % 4 if h else n))
+            def _():
+                copy = hop(c, h, ab, u)
+                if n > 0:
+                    copy.wait_recv()
+                if n < 3:
+                    copy.start()
+            if n < 3:
+                moved.append((c, h, ab, u, n))
+
+    def zwait(u):
+        for copy in f_z[u]:
+            copy.wait_recv()
+
+    def dview(c, q):
+        return db.at[pl.ds(2 * c, 8 - 2 * c), q, :, pl.ds(c * wide, wide)]
+
+    def d1(c):
+        if c == CHUNKS - 1:
+            d_own.wait()
+            for copy in d_r:
+                copy.wait_recv()
+        src = dview(c, piece)
+        done["dz", c] = remote(src, src, {"zl": 1 - zl})
+
+    def d2(c):
+        done["dz", c].wait_recv()
+        src = dview(c, pl.ds(2 * y, 2))
+        done["dy", c] = [remote(src, src, {"y": yp}), remote(src, src, {"y": ym})]
+
+    def d3(c):
+        for copy in done["dy", c]:
+            copy.wait_recv()
+        low, high = dview(c, 2 * ym), dview(c, 2 * yp + 1)
+        done["dy2", c] = [remote(low, low, {"y": yp}), remote(high, high, {"y": ym})]
+
+    def d4(c):
+        for copy in done["dy2", c]:
+            copy.wait_recv()
+
+    def base():
+        f_own.wait()
+        f_k.wait_recv()
+        l_own.wait()
+        l_k.wait_recv()
 
     block = 512
     steps = rows // block
-    done = {}
 
     def slab(b):
         return pl.ds(al(b * pair, pair), pair)
@@ -273,16 +333,32 @@
                 )
             cb[m, :] = acc
 
-    c_own.wait()
     stages = [s1, s2, s3, s4, s5, s6, s7, s8, s9]
-    order = sorted(
-        (turn * SPREAD + n, n, CHUNKS - 1 - turn) for turn in range(CHUNKS) for n in range(len(stages))
-    )
-    for _, n, c in order:
-        stages[n](c)
+    plan = [(START - 0.1, base, ()), (START + TIMES[8] - 0.1, c_own.wait, ())]
+    for u in range(SUB):
+        plan.append((8.0 + 2.0 * u, zwait, (u,)))
+    for turn in range(CHUNKS):
+        c = CHUNKS - 1 - turn
+        for n, step in enumerate((d1, d2, d3, d4)):
+            plan.append((5.5 + 3.5 * n + 2.0 * turn, step, (c,)))
+        for u in range(SUB):
+            for ab in range(2):
+                for n in range(4):
+                    when = (8.0 + 0.1 if ab else 2.0) + 2.0 * u + 4.0 * n + 2.0 * turn
+                    plan.append((when, relay, (c, ab, u, n)))
+        last = max(when for when, step, args in plan if step in (relay, d4) and args[0] == c)
+        begin = max(START + PERIOD * turn, last + 0.01)
+        for n, step in enumerate(stages):
+            plan.append((begin + TIMES[n], step, (c,)))
+    for when, step, args in sorted(plan, key=lambda item: item[0]):
+        step(*args)
     result = here(cb, out_ref)
-    for copy in sent:
+    for copy in sent + f_a:
         copy.wait_send()
+    for c, h, ab, u, n in moved:
+        @pl.when(when_at(c, (4 - n) % 4 if h else n))
+        def _():
+            hop(c, h, ab, u).wait_send()
     for c in range(CHUNKS):
         @pl.when(jnp.logical_not(diagonal))
         def _():
@@ -300,7 +376,7 @@
         drows, width = inverses.shape[1:]
         wide = width // CHUNKS
         part = rows // 8
-        n_remote = 19 + 2 + 1 + 2 + 2 + 2 + 19 * CHUNKS
+        n_remote = 9 + 2 * SUB + 23 * CHUNKS
         return pl.pallas_call(
             kernel,
             out_shape=jax.ShapeDtypeStruct(covariance.shape, covariance.dtype),
@@ -321,6 +397,9 @@
                 pltpu.VMEM((rows, cols), F32),
                 pltpu.SemaphoreType.DMA((n_remote,)),
                 pltpu.SemaphoreType.DMA((n_remote,)),
+                pltpu.SemaphoreType.DMA((16 * SUB,)),
+                pltpu.SemaphoreType.DMA((16 * SUB,)),
+                pltpu.SemaphoreType.DMA((2 * SUB,)),
                 pltpu.SemaphoreType.DMA((8,)),
             ],
             compiler_params=pltpu.CompilerParams(

time: 150 us -> 128 us (0.85)
  Pallas kernels: 145 us -> 123 us
    pallas_call x1, Pallas kernels: 145 us -> 123 us  [body(): pl.pallas_call(kernel, out_shape=jax.ShapeDtypeStruct(covariance.shape, c...]
where the time goes in v2:
time: 128 us
  Pallas kernels  123 us (96%)
  local copies, waits for them, and re-layouts  4.83 us (4%)
    pallas_call x1, Pallas kernels, body(): pl.pallas_call(kernel, out_shape=jax.ShapeDtypeStruct(covariance.shape, c...  123 us
    unnamed x1, local copies, waits for them, and re-layouts  4.83 us

profile of v2, /device:TPU:1, one launch (start us, length us, event | category | flops | bytes accessed | tf_op | source)
XLA Modules:
  0.0 127.6 jit_solution(9541570994736529663)
XLA Ops:
  0.0 122.8 %shard_map.46 = f32[1536,768]{1,0:T(8,128)} custom-call(bf16[1536,768]{1,0:T(8,128)(2,1)} %l_ref.1, bf16[2,768,128]{2,1,0:T(8,128)(2,1)} %f_ref.1, bf16[2,128,1024]{2,1,0:T(8,128)(2,1)} %d_ref.1, f32[1536,768]{1,0:T(8,128)} %c_ref.1), custom_call_target="tpu_custom_call" | custom-call | tf_op jit(solution)/shard_map/pallas_call | solution.py:380
  122.8 4.8 %copy.6 = f32[1536,768]{1,0:T(8,128)} copy(f32[1536,768]{1,0:T(8,128)} %shard_map.46) | data formatting | bytes 9437184

commit v3 on v2

--- a/solution.py
+++ b/solution.py
@@ -13,8 +13,19 @@
 
 CHUNKS = 4
 SUB = 2
-START, PERIOD = 20.0, 2.7
-TIMES = (0.0, 2.8, 5.6, 8.4, 11.2, 13.9, 16.6, 19.3, 22.0)
+ORDER = (
+    (1,0), (0,0,0,1,1), (0,1,0,0,1), (0,2,0,0,1), (0,1,0,1,1), (0,3,0,0,1), (0,0,0,0,1), (0,2,0,1,1), (0,2,1,0,0),
+    (1,1), (0,1,1,0,0), (0,3,0,1,1), (0,0,1,0,0), (0,3,1,1,0), (0,3,0,0,2), (0,2,0,0,2), (0,2,1,1,0), (0,1,0,0,2),
+    (0,3,1,0,0), (0,0,0,0,2), (0,2,0,1,2), (0,1,1,0,1), (0,2,1,1,1), (0,0,1,1,0), (0,0,0,1,2), (0,1,1,1,0),
+    (0,1,0,1,2), (0,3,1,0,1), (0,0,1,0,1), (3,1), (3,2), (0,3,0,1,2), (3,0), (3,3), (0,2,1,0,1), (0,2,0,0,3),
+    (0,1,1,1,1), (0,3,1,1,1), (4,1), (0,0,1,1,1), (0,1,1,1,2), (0,2,1,1,2), (0,0,0,0,3), (0,3,0,0,3), (4,2),
+    (0,2,1,0,2), (0,0,1,0,2), (0,1,1,0,2), (0,3,1,0,2), (0,3,1,1,2), (4,0), (4,3), (0,0,1,1,2), (0,1,1,1,3),
+    (0,3,1,0,3), (0,1,0,0,3), (0,0,1,0,3), (0,2,1,1,3), (0,3,1,1,3), (5,1), (0,2,0,1,3), (0,3,0,1,3), (0,1,1,0,3),
+    (0,1,0,1,3), (0,2,1,0,3), (0,0,0,1,3), (5,2), (6,2), (6,1), (5,3), (0,0,1,1,3), (7,2), (5,0), (7,1), (6,0),
+    (8,2), (6,3), (8,1), (7,0), (9,2), (9,1), (11,2), (7,3), (8,0), (11,1), (10,1), (13,2), (10,2), (8,3), (9,0),
+    (13,1), (9,3), (10,3), (15,2), (11,0), (12,1), (15,1), (11,3), (10,0), (13,0), (13,3), (12,0), (16,2), (15,0),
+    (16,1), (12,2), (14,1), (15,3), (14,0), (17,1), (14,2), (12,3), (16,0), (16,3), (17,2), (14,3), (17,0), (17,3),
+)
 
 
 def al(i, n):
@@ -22,8 +33,8 @@
 
 
 def kernel(
-    l_ref, f_ref, d_ref, c_ref, out_ref,
-    lb, g, db, s, t, own, rs1, rs2, rsz, ir, iq, cb, send, recv, send_f, recv_f, send_a, local,
+    l_ref, f_ref, d_ref, c_ref, cb, irl_ref, iql_ref,
+    lb, g, db, s, t, own, rs1, rs2, rsz, ir, iq, send, recv, send_f, recv_f, send_a, send_d, recv_d, local_d, send_x, recv_x, local,
 ):
     zl, x, zh, y, k = (lax.axis_index(a) for a in AXES)
     rows, cols = l_ref.shape
@@ -49,11 +60,12 @@
     bx = lax.rem(y + d_from, 4)
     bxp, bxm = lax.rem(bx + 1, 4), lax.rem(bx + 3, 4)
 
+    shifts = [(dx, dz) for dx in range(4) for dz in range(2) if dx or dz]
     group = [
-        {"x": lax.rem(x + dx, 4), "zh": lax.rem(zh + dz, 2)}
-        for dx in range(4) for dz in range(2) if dx or dz
+        {"x": lax.rem(x + dx, 4), "zh": lax.rem(zh + dz, 2), "zl": lax.rem(zl + dz, 2)} for dx, dz in shifts
     ]
     peers = group + [
+        {"zh": 1 - zh},
         {"k": 1 - k}, {"zh": 1 - zh, "k": 1 - k}, {"x": xp, "k": 1 - k}, {"x": xm, "k": 1 - k},
         {"zl": 1 - zl}, {"y": yp}, {"y": ym},
     ]
@@ -71,6 +83,10 @@
     def _():
         pl.semaphore_wait(barrier, len(peers))
 
+    final = [entry for entry in ORDER if entry[0] == 17][-1][1]
+    irs = {c: ir.at[:, n] for n, c in enumerate(c for c in range(CHUNKS) if c != final)}
+    iqs = {c: iq.at[:, n] for n, c in enumerate(c for c in range(CHUNKS) if c != final)}
+    irs[final], iqs[final] = irl_ref, iql_ref
     counts = {"remote": 0, "local": 0}
     sent = []
 
@@ -92,10 +108,26 @@
         copy.start()
         return copy
 
-    dpart = drows // 8
-    dsrc = d_ref.at[k, pl.ds(al(piece * dpart, dpart), dpart), :]
-    d_own = here(dsrc, db.at[r, piece])
-    d_r = [remote(dsrc, db.at[r, piece], peer) for peer in group]
+    dpart = drows // 4
+
+    def d_copy(c, n):
+        lanes = pl.ds(c * wide, wide)
+        src = d_ref.at[k, pl.ds(al(y * dpart, dpart), dpart), lanes]
+        dst = db.at[r, y, :, lanes]
+        if n < 0:
+            return pltpu.make_async_copy(src, dst, local_d.at[c])
+        return pltpu.make_async_remote_copy(
+            src_ref=src, dst_ref=dst, send_sem=send_d.at[c, n], recv_sem=recv_d.at[c, n],
+            device_id=group[n], device_id_type=MESH,
+        )
+
+    def d_spread(c):
+        @pl.when(x >= c)
+        def _():
+            for n in range(-1, len(group)):
+                d_copy(c, n).start()
+
+    d_spread(CHUNKS - 1)
 
     sub = cols // SUB
 
@@ -143,49 +175,76 @@
     l_k = remote(l_ref, lb.at[k], {"k": 1 - k})
     c_own = here(c_ref, cb)
     done = {}
-    moved = []
 
     def when_at(c, n):
         return lax.rem(x - c + 4, 4) == n
 
+    def across(c, h, u):
+        n = (c * 2 + h) * SUB + u
+        ref = g.at[c, rows_f(h, u), lanes_f(zh)]
+        return pltpu.make_async_remote_copy(
+            src_ref=ref, dst_ref=ref, send_sem=send_x.at[n], recv_sem=recv_x.at[n],
+            device_id={"zh": 1 - zh}, device_id_type=MESH,
+        )
+
     def relay(c, ab, u, n):
-        for h in range(2):
-            if n == 0 and ab == 0:
-                continue
-            @pl.when(when_at(c, (4 - n) % 4 if h else n))
-            def _():
-                copy = hop(c, h, ab, u)
-                if n > 0:
+        if ab == 0:
+            for h in range(2):
+                @pl.when(when_at(c, (4 - n) % 4 if h else n))
+                def _():
+                    copy = hop(c, h, 0, u)
                     copy.wait_recv()
-                if n < 3:
-                    copy.start()
-            if n < 3:
-                moved.append((c, h, ab, u, n))
+                    if n < 3:
+                        copy.start()
+            return
+
+        at = when_at(c, 0) if n == 0 else when_at(c, 2)
+        if n == 3:
+            at = jnp.logical_or(when_at(c, 1), when_at(c, 3))
+
+        @pl.when(at)
+        def _():
+            for h in range(2):
+                if n == 1:
+                    across(c, h, u).start()
+                    continue
+                if n == 2:
+                    across(c, h, u).wait_recv()
+                if n == 3:
+                    hop(c, h, 1, u).wait_recv()
+                else:
+                    hop(c, h, 1, u).start()
 
     def zwait(u):
         for copy in f_z[u]:
             copy.wait_recv()
 
-    def dview(c, q):
-        return db.at[pl.ds(2 * c, 8 - 2 * c), q, :, pl.ds(c * wide, wide)]
+    for c in range(CHUNKS - 2, -1, -1):
+        d_spread(c)
+
+    def dview(c, q, rows_d):
+        return db.at[pl.ds(2 * c, 8 - 2 * c), q, rows_d, pl.ds(c * wide, wide)]
 
     def d1(c):
-        if c == CHUNKS - 1:
-            d_own.wait()
-            for copy in d_r:
-                copy.wait_recv()
-        src = dview(c, piece)
-        done["dz", c] = remote(src, src, {"zl": 1 - zl})
+        pass
 
     def d2(c):
-        done["dz", c].wait_recv()
-        src = dview(c, pl.ds(2 * y, 2))
+        @pl.when(x >= c)
+        def _():
+            d_copy(c, -1).wait()
+
+        for n, (dx, _) in enumerate(shifts):
+            @pl.when(lax.rem(x - dx + 4, 4) >= c)
+            def _():
+                d_copy(c, n).wait_recv()
+        src = dview(c, y, pl.ds(0, dpart))
         done["dy", c] = [remote(src, src, {"y": yp}), remote(src, src, {"y": ym})]
 
     def d3(c):
         for copy in done["dy", c]:
             copy.wait_recv()
-        low, high = dview(c, 2 * ym), dview(c, 2 * yp + 1)
+        half = dpart // 2
+        low, high = dview(c, ym, pl.ds(0, half)), dview(c, yp, pl.ds(half, half))
         done["dy2", c] = [remote(low, low, {"y": yp}), remote(high, high, {"y": ym})]
 
     def d4(c):
@@ -257,12 +316,12 @@
 
     def s4(c):
         done["rsz", c].wait_recv()
-        ir[k, c, thin(piece), :] = (-(own[c] + rsz[c, 1].astype(F32))).astype(BF16)
-        src = ir.at[k, c, thin(piece)]
+        irs[c][k, thin(piece), :] = (-(own[c] + rsz[c, 1].astype(F32))).astype(BF16)
+        src = irs[c].at[k, thin(piece)]
         done["agz", c] = remote(src, src, {"zl": 1 - zl})
         n = counts["remote"]
         counts["remote"] += 1
-        dst = iq.at[k, c, thin(piece)]
+        dst = iqs[c].at[k, thin(piece)]
         away = pltpu.make_async_remote_copy(
             src_ref=src, dst_ref=dst, send_sem=send.at[n], recv_sem=recv.at[n], device_id=tr_to, device_id_type=MESH
         )
@@ -277,10 +336,12 @@
         def _():
             still.start()
 
-    def s5(c):
+    def s5a(c):
         done["agz", c].wait_recv()
-        src = ir.at[k, c, slab(y)]
+        src = irs[c].at[k, slab(y)]
         done["agy", c] = [remote(src, src, {"y": yp}), remote(src, src, {"y": ym})]
+
+    def s5b(c):
         away, still = done["tr", c]
 
         @pl.when(jnp.logical_not(diagonal))
@@ -291,31 +352,35 @@
         def _():
             still.wait()
 
-        src = iq.at[k, c, thin(got)]
+        src = iqs[c].at[k, thin(got)]
         done["cgz", c] = remote(src, src, {"zh": 1 - zh})
 
-    def s6(c):
+    def s6a(c):
         for copy in done["agy", c]:
             copy.wait_recv()
-        low, high = ir.at[k, c, thin(2 * ym)], ir.at[k, c, thin(2 * yp + 1)]
+        low, high = irs[c].at[k, thin(2 * ym)], irs[c].at[k, thin(2 * yp + 1)]
         done["agy2", c] = [remote(low, low, {"y": yp}), remote(high, high, {"y": ym})]
+
+    def s6b(c):
         done["cgz", c].wait_recv()
-        src = iq.at[k, c, slab(bx)]
+        src = iqs[c].at[k, slab(bx)]
         done["cgx", c] = [remote(src, src, {"x": xp}), remote(src, src, {"x": xm})]
 
-    def s7(c):
+    def s7a(c):
         for copy in done["agy2", c]:
             copy.wait_recv()
-        done["ir", c] = remote(ir.at[k, c], ir.at[k, c], {"k": 1 - k})
+        done["ir", c] = remote(irs[c].at[k], irs[c].at[k], {"k": 1 - k})
+
+    def s7b(c):
         for copy in done["cgx", c]:
             copy.wait_recv()
-        low, high = iq.at[k, c, thin(2 * bxm)], iq.at[k, c, thin(2 * bxp + 1)]
+        low, high = iqs[c].at[k, thin(2 * bxm)], iqs[c].at[k, thin(2 * bxp + 1)]
         done["cgx2", c] = [remote(low, low, {"x": xp}), remote(high, high, {"x": xm})]
 
     def s8(c):
         for copy in done["cgx2", c]:
             copy.wait_recv()
-        src = iq.at[k, c, pl.ds(al((1 - k) * cols, cols), cols)]
+        src = iqs[c].at[k, pl.ds(al((1 - k) * cols, cols), cols)]
         done["iq", c] = remote(src, src, {"k": 1 - k})
 
     def s9(c):
@@ -328,42 +393,70 @@
             acc = cb[m, :]
             for p in range(2):
                 acc += lax.dot_general(
-                    ir[p, c, m, :], iq[p, c, pl.ds(al(k * cols, cols), cols), :],
+                    irs[c][p, m, :], iqs[c][p, pl.ds(al(k * cols, cols), cols), :],
                     (((1,), (1,)), ((), ())), preferred_element_type=F32,
                 )
             cb[m, :] = acc
 
-    stages = [s1, s2, s3, s4, s5, s6, s7, s8, s9]
-    plan = [(START - 0.1, base, ()), (START + TIMES[8] - 0.1, c_own.wait, ())]
-    for u in range(SUB):
-        plan.append((8.0 + 2.0 * u, zwait, (u,)))
-    for turn in range(CHUNKS):
-        c = CHUNKS - 1 - turn
-        for n, step in enumerate((d1, d2, d3, d4)):
-            plan.append((5.5 + 3.5 * n + 2.0 * turn, step, (c,)))
-        for u in range(SUB):
-            for ab in range(2):
-                for n in range(4):
-                    when = (8.0 + 0.1 if ab else 2.0) + 2.0 * u + 4.0 * n + 2.0 * turn
-                    plan.append((when, relay, (c, ab, u, n)))
-        last = max(when for when, step, args in plan if step in (relay, d4) and args[0] == c)
-        begin = max(START + PERIOD * turn, last + 0.01)
-        for n, step in enumerate(stages):
-            plan.append((begin + TIMES[n], step, (c,)))
-    for when, step, args in sorted(plan, key=lambda item: item[0]):
+    steps_of = (relay, zwait, d1, d2, d3, d4, s1, s2, s3, s4, s5a, s5b, s6a, s6b, s7a, s7b, s8, s9)
+    based = False
+    added = []
+    for entry in ORDER:
+        step, args = steps_of[entry[0]], entry[1:]
+        if step is s1 and not based:
+            base()
+            based = True
+        if step is s9 and not added:
+            c_own.wait()
+        if step is s9:
+            added.append(args[0])
+            if len(added) == CHUNKS:
+                break
         step(*args)
-    result = here(cb, out_ref)
+    done["ir", final].wait_recv()
+    done["iq", final].wait_recv()
     for copy in sent + f_a:
         copy.wait_send()
-    for c, h, ab, u, n in moved:
-        @pl.when(when_at(c, (4 - n) % 4 if h else n))
-        def _():
-            hop(c, h, ab, u).wait_send()
+    for c in range(CHUNKS):
+        @pl.when(x >= c)
+        def _():
+            for n in range(len(group)):
+                d_copy(c, n).wait_send()
+
+        for u in range(SUB):
+            for n in range(1, 3):
+                for h in range(2):
+                    @pl.when(when_at(c, (4 - n) % 4 if h else n))
+                    def _():
+                        hop(c, h, 0, u).wait_send()
+
+            @pl.when(when_at(c, 0))
+            def _():
+                for h in range(2):
+                    hop(c, h, 1, u).wait_send()
+
+            @pl.when(when_at(c, 2))
+            def _():
+                for h in range(2):
+                    across(c, h, u).wait_send()
+                    hop(c, h, 1, u).wait_send()
+
     for c in range(CHUNKS):
         @pl.when(jnp.logical_not(diagonal))
         def _():
             done["tr", c][0].wait_send()
-    result.wait()
+
+
+def last(c_ref, ir_ref, iq_ref, out_ref):
+    tall, cols = out_ref.shape
+    block = pl.ds(al(lax.axis_index("k") * cols, cols), cols)
+    m = pl.ds(al(pl.program_id(0) * tall, tall), tall)
+    total = c_ref[m, :]
+    for p in range(2):
+        total += lax.dot_general(
+            ir_ref[p, m, :], iq_ref[p, block, :], (((1,), (1,)), ((), ())), preferred_element_type=F32
+        )
+    out_ref[...] = total
 
 
 def solution(mesh):
@@ -376,36 +469,53 @@
         drows, width = inverses.shape[1:]
         wide = width // CHUNKS
         part = rows // 8
-        n_remote = 9 + 2 * SUB + 23 * CHUNKS
-        return pl.pallas_call(
+        n_remote = 2 + 2 * SUB + 22 * CHUNKS
+        partial_sum, left, right = pl.pallas_call(
             kernel,
-            out_shape=jax.ShapeDtypeStruct(covariance.shape, covariance.dtype),
-            in_specs=[pl.BlockSpec(memory_space=pl.ANY)] * 4,
-            out_specs=pl.BlockSpec(memory_space=pl.ANY),
+            out_shape=[
+                pltpu.VMEM((rows, cols), F32),
+                pltpu.VMEM((2, rows, wide), BF16),
+                pltpu.VMEM((2, 2 * cols, wide), BF16),
+            ],
+            in_specs=[pl.BlockSpec(memory_space=pltpu.HBM)] * 4,
+            out_specs=[pl.BlockSpec(memory_space=pltpu.VMEM)] * 3,
             scratch_shapes=[
                 pltpu.VMEM((2, rows, cols), BF16),
                 pltpu.VMEM((4, 2 * cols, 2 * fcols), BF16),
-                pltpu.VMEM((8, 8, drows // 8, width), BF16),
+                pltpu.VMEM((8, 4, drows // 4, width), BF16),
                 pltpu.VMEM((2 * cols, wide), BF16),
                 pltpu.VMEM((CHUNKS, rows, wide), BF16),
                 pltpu.VMEM((CHUNKS, part, wide), F32),
                 pltpu.VMEM((CHUNKS, 2, part, wide), BF16),
                 pltpu.VMEM((CHUNKS, 2, 2 * part, wide), BF16),
                 pltpu.VMEM((CHUNKS, 2, part, wide), BF16),
-                pltpu.VMEM((2, CHUNKS, rows, wide), BF16),
-                pltpu.VMEM((2, CHUNKS, rows, wide), BF16),
-                pltpu.VMEM((rows, cols), F32),
+                pltpu.VMEM((2, CHUNKS - 1, rows, wide), BF16),
+                pltpu.VMEM((2, CHUNKS - 1, rows, wide), BF16),
                 pltpu.SemaphoreType.DMA((n_remote,)),
                 pltpu.SemaphoreType.DMA((n_remote,)),
                 pltpu.SemaphoreType.DMA((16 * SUB,)),
                 pltpu.SemaphoreType.DMA((16 * SUB,)),
                 pltpu.SemaphoreType.DMA((2 * SUB,)),
+                pltpu.SemaphoreType.DMA((CHUNKS, 7)),
+                pltpu.SemaphoreType.DMA((CHUNKS, 7)),
+                pltpu.SemaphoreType.DMA((CHUNKS,)),
+                pltpu.SemaphoreType.DMA((8 * SUB,)),
+                pltpu.SemaphoreType.DMA((8 * SUB,)),
                 pltpu.SemaphoreType.DMA((8,)),
             ],
             compiler_params=pltpu.CompilerParams(
-                collective_id=0, has_side_effects=True, vmem_limit_bytes=60 * 1024 * 1024
+                collective_id=0, has_side_effects=True, vmem_limit_bytes=50 * 1024 * 1024
             ),
         )(held, factor, inverses, covariance)
+        tall = 256
+        return pl.pallas_call(
+            last,
+            out_shape=jax.ShapeDtypeStruct(covariance.shape, covariance.dtype),
+            grid=(rows // tall,),
+            in_specs=[pl.BlockSpec(memory_space=pltpu.VMEM)] * 3,
+            out_specs=pl.BlockSpec((tall, cols), lambda i: (i, 0)),
+            compiler_params=pltpu.CompilerParams(vmem_limit_bytes=8 * 1024 * 1024),
+        )(partial_sum, left, right)
 
     spec = P(("x", "zh"), ("zl", "y", "k"))
     return jax.shard_map(

time: 128 us -> 122 us (0.953)
  local copies, waits for them, and re-layouts: 4.83 us -> 0 us
    unnamed x1 -> x0, local copies, waits for them, and re-layouts: 4.83 us -> none
    pallas_call x1 -> x2, Pallas kernels: 123 us -> 122 us  [the longest x1 118 us: body(): pl.pallas_call(kernel, out_shape=[pltpu.VMEM((rows, cols), F32), pltpu.VM...]
where the time goes in v3:
time: 122 us
  Pallas kernels  122 us (100%)
    pallas_call x1, Pallas kernels, body(): pl.pallas_call(kernel, out_shape=[pltpu.VMEM((rows, cols), F32), pltpu.VM...  118 us
    pallas_call x1, Pallas kernels, body(): pl.pallas_call(last, out_shape=jax.ShapeDtypeStruct(covariance.shape, cov...  4.3 us

profile of v3, /device:TPU:1, one launch (start us, length us, event | category | flops | bytes accessed | tf_op | source)
XLA Modules:
  0.0 122.2 jit_solution(13522148516826868678)
XLA Ops:
  0.0 117.9 %shard_map.46 = (f32[1536,768]{1,0:T(8,128)S(1)}, bf16[2,1536,256]{2,1,0:T(8,128)(2,1)S(1)}, bf16[2,1536,256]{2,1,0:T(8,128)(2,1)S(1)}) custom-call(bf16[1536,768]{1,0:T(8,128)(2,1)} %l_ref.1, bf16[2,768,128]{2,1,0:T(8,128)(2,1)} %f_ref.1, bf16[2,128,1024]{2,1,0:T(8,128)(2,1)} %d_ref.1, f32[1536,768]{1,0:T(8,128)} %c_ref.1), custom_call_target="tpu_custom_call" | custom-call | tf_op jit(solution)/shard_map/pallas_call | solution.py:473
  117.9 4.3 %shard_map.47 = f32[1536,768]{1,0:T(8,128)} custom-call(f32[1536,768]{1,0:T(8,128)S(1)} %get-tuple-element.8.c_ref, bf16[2,1536,256]{2,1,0:T(8,128)(2,1)S(1)} %get-tuple-element.9.ir_ref, bf16[2,1536,256]{2,1,0:T(8,128)(2,1)S(1)} %get-tuple-element.10.iq_ref), custom_call_target="tpu_custom_call" | custom-call | tf_op jit(solution)/shard_map/pallas_call | solution.py:511

commit v4 on v3

--- a/solution.py
+++ b/solution.py
@@ -14,17 +14,17 @@
 CHUNKS = 4
 SUB = 2
 ORDER = (
-    (1,0), (0,0,0,1,1), (0,1,0,0,1), (0,2,0,0,1), (0,1,0,1,1), (0,3,0,0,1), (0,0,0,0,1), (0,2,0,1,1), (0,2,1,0,0),
-    (1,1), (0,1,1,0,0), (0,3,0,1,1), (0,0,1,0,0), (0,3,1,1,0), (0,3,0,0,2), (0,2,0,0,2), (0,2,1,1,0), (0,1,0,0,2),
-    (0,3,1,0,0), (0,0,0,0,2), (0,2,0,1,2), (0,1,1,0,1), (0,2,1,1,1), (0,0,1,1,0), (0,0,0,1,2), (0,1,1,1,0),
-    (0,1,0,1,2), (0,3,1,0,1), (0,0,1,0,1), (3,1), (3,2), (0,3,0,1,2), (3,0), (3,3), (0,2,1,0,1), (0,2,0,0,3),
-    (0,1,1,1,1), (0,3,1,1,1), (4,1), (0,0,1,1,1), (0,1,1,1,2), (0,2,1,1,2), (0,0,0,0,3), (0,3,0,0,3), (4,2),
-    (0,2,1,0,2), (0,0,1,0,2), (0,1,1,0,2), (0,3,1,0,2), (0,3,1,1,2), (4,0), (4,3), (0,0,1,1,2), (0,1,1,1,3),
-    (0,3,1,0,3), (0,1,0,0,3), (0,0,1,0,3), (0,2,1,1,3), (0,3,1,1,3), (5,1), (0,2,0,1,3), (0,3,0,1,3), (0,1,1,0,3),
-    (0,1,0,1,3), (0,2,1,0,3), (0,0,0,1,3), (5,2), (6,2), (6,1), (5,3), (0,0,1,1,3), (7,2), (5,0), (7,1), (6,0),
-    (8,2), (6,3), (8,1), (7,0), (9,2), (9,1), (11,2), (7,3), (8,0), (11,1), (10,1), (13,2), (10,2), (8,3), (9,0),
-    (13,1), (9,3), (10,3), (15,2), (11,0), (12,1), (15,1), (11,3), (10,0), (13,0), (13,3), (12,0), (16,2), (15,0),
-    (16,1), (12,2), (14,1), (15,3), (14,0), (17,1), (14,2), (12,3), (16,0), (16,3), (17,2), (14,3), (17,0), (17,3),
+    (0,1,0,0,1), (0,0,0,0,1), (0,0,0,1,1), (0,2,0,0,1), (1,0), (0,3,1,0,0), (0,1,1,0,0), (0,1,0,0,2), (0,3,0,0,1),
+    (0,1,0,1,1), (0,2,0,1,1), (0,1,0,1,2), (1,1), (0,1,1,1,0), (0,3,0,1,1), (0,3,0,0,2), (0,3,1,0,1), (0,0,0,1,2),
+    (0,2,0,0,2), (0,0,0,0,2), (0,2,1,1,0), (3,1), (0,0,1,1,0), (0,3,0,1,2), (0,2,1,0,0), (0,3,1,1,0), (0,0,1,1,1),
+    (0,1,1,1,1), (3,0), (0,0,0,1,3), (0,0,1,0,0), (3,2), (0,0,1,0,1), (0,2,1,0,1), (0,1,1,0,1), (0,3,1,1,1),
+    (0,2,1,0,2), (0,2,0,0,3), (3,3), (4,1), (0,3,1,0,2), (0,2,0,1,2), (0,1,1,1,2), (4,0), (0,3,1,1,2), (0,3,0,0,3),
+    (0,1,0,0,3), (0,2,1,0,3), (0,2,1,1,1), (0,1,1,1,3), (0,0,1,0,2), (0,3,1,0,3), (0,0,1,1,2), (0,1,1,0,2), (4,3),
+    (5,1), (0,0,0,0,3), (0,2,1,1,2), (0,1,0,1,3), (5,3), (4,2), (0,1,1,0,3), (0,3,1,1,3), (0,2,0,1,3), (0,3,0,1,3),
+    (6,3), (0,0,1,0,3), (0,2,1,1,3), (5,2), (6,2), (7,3), (6,1), (5,0), (0,0,1,1,3), (7,2), (7,1), (8,3), (6,0),
+    (8,2), (9,3), (9,2), (8,1), (7,0), (11,3), (9,1), (8,0), (10,2), (11,2), (13,3), (10,1), (9,0), (15,3), (11,1),
+    (10,3), (10,0), (13,2), (13,1), (11,0), (12,2), (15,2), (12,3), (12,1), (16,3), (13,0), (16,2), (15,1), (14,2),
+    (12,0), (14,3), (14,1), (15,0), (17,3), (16,1), (14,0), (17,2), (16,0), (17,1), (17,0),
 )
 
 

time: 122 us -> 118 us (0.967)
  Pallas kernels: 122 us -> 117 us
    pallas_call x1, Pallas kernels: 118 us -> 113 us  [body(): pl.pallas_call(kernel, out_shape=[pltpu.VMEM((rows, cols), F32), pltpu.VM...]
where the time goes in v4:
time: 118 us; the launch traced here: 117 us
  Pallas kernels  117 us (99%)
    pallas_call x1, Pallas kernels, body(): pl.pallas_call(kernel, out_shape=[pltpu.VMEM((rows, cols), F32), pltpu.VM...  113 us
    pallas_call x1, Pallas kernels, body(): pl.pallas_call(last, out_shape=jax.ShapeDtypeStruct(covariance.shape, cov...  4.3 us

profile of v4, /device:TPU:1, one launch (start us, length us, event | category | flops | bytes accessed | tf_op | source)
XLA Modules:
  0.0 117.4 jit_solution(10109508424316233127)
XLA Ops:
  0.0 113.1 %shard_map.46 = (f32[1536,768]{1,0:T(8,128)S(1)}, bf16[2,1536,256]{2,1,0:T(8,128)(2,1)S(1)}, bf16[2,1536,256]{2,1,0:T(8,128)(2,1)S(1)}) custom-call(bf16[1536,768]{1,0:T(8,128)(2,1)} %l_ref.1, bf16[2,768,128]{2,1,0:T(8,128)(2,1)} %f_ref.1, bf16[2,128,1024]{2,1,0:T(8,128)(2,1)} %d_ref.1, f32[1536,768]{1,0:T(8,128)} %c_ref.1), custom_call_target="tpu_custom_call" | custom-call | tf_op jit(solution)/shard_map/pallas_call | solution.py:473
  113.1 4.3 %shard_map.47 = f32[1536,768]{1,0:T(8,128)} custom-call(f32[1536,768]{1,0:T(8,128)S(1)} %get-tuple-element.8.c_ref, bf16[2,1536,256]{2,1,0:T(8,128)(2,1)S(1)} %get-tuple-element.9.ir_ref, bf16[2,1536,256]{2,1,0:T(8,128)(2,1)S(1)} %get-tuple-element.10.iq_ref), custom_call_target="tpu_custom_call" | custom-call | tf_op jit(solution)/shard_map/pallas_call | solution.py:511

commit v5 on v4

--- a/solution.py
+++ b/solution.py
@@ -13,18 +13,19 @@
 
 CHUNKS = 4
 SUB = 2
+LAST = 8
 ORDER = (
-    (0,1,0,0,1), (0,0,0,0,1), (0,0,0,1,1), (0,2,0,0,1), (1,0), (0,3,1,0,0), (0,1,1,0,0), (0,1,0,0,2), (0,3,0,0,1),
-    (0,1,0,1,1), (0,2,0,1,1), (0,1,0,1,2), (1,1), (0,1,1,1,0), (0,3,0,1,1), (0,3,0,0,2), (0,3,1,0,1), (0,0,0,1,2),
-    (0,2,0,0,2), (0,0,0,0,2), (0,2,1,1,0), (3,1), (0,0,1,1,0), (0,3,0,1,2), (0,2,1,0,0), (0,3,1,1,0), (0,0,1,1,1),
-    (0,1,1,1,1), (3,0), (0,0,0,1,3), (0,0,1,0,0), (3,2), (0,0,1,0,1), (0,2,1,0,1), (0,1,1,0,1), (0,3,1,1,1),
-    (0,2,1,0,2), (0,2,0,0,3), (3,3), (4,1), (0,3,1,0,2), (0,2,0,1,2), (0,1,1,1,2), (4,0), (0,3,1,1,2), (0,3,0,0,3),
-    (0,1,0,0,3), (0,2,1,0,3), (0,2,1,1,1), (0,1,1,1,3), (0,0,1,0,2), (0,3,1,0,3), (0,0,1,1,2), (0,1,1,0,2), (4,3),
-    (5,1), (0,0,0,0,3), (0,2,1,1,2), (0,1,0,1,3), (5,3), (4,2), (0,1,1,0,3), (0,3,1,1,3), (0,2,0,1,3), (0,3,0,1,3),
-    (6,3), (0,0,1,0,3), (0,2,1,1,3), (5,2), (6,2), (7,3), (6,1), (5,0), (0,0,1,1,3), (7,2), (7,1), (8,3), (6,0),
-    (8,2), (9,3), (9,2), (8,1), (7,0), (11,3), (9,1), (8,0), (10,2), (11,2), (13,3), (10,1), (9,0), (15,3), (11,1),
-    (10,3), (10,0), (13,2), (13,1), (11,0), (12,2), (15,2), (12,3), (12,1), (16,3), (13,0), (16,2), (15,1), (14,2),
-    (12,0), (14,3), (14,1), (15,0), (17,3), (16,1), (14,0), (17,2), (16,0), (17,1), (17,0),
+    (0,2,0,1,1), (0,1,0,0,1), (0,0,0,1,1), (0,1,0,1,1), (0,3,0,0,1), (1,0), (0,2,0,0,1), (0,3,0,0,2), (0,3,0,1,1),
+    (0,3,1,0,0), (0,3,1,0,1), (0,2,0,1,2), (0,0,0,0,1), (3,3), (1,1), (0,1,1,0,0), (0,1,0,0,2), (0,2,1,0,0),
+    (0,3,1,1,0), (0,0,0,1,2), (3,1), (0,0,1,0,0), (0,2,1,1,0), (3,2), (0,1,1,0,1), (0,3,0,1,2), (0,1,1,1,0),
+    (0,2,1,1,1), (0,0,1,1,0), (0,2,0,0,2), (0,1,0,1,2), (3,0), (0,1,1,1,1), (0,0,1,1,1), (0,3,1,1,1), (0,2,1,0,1),
+    (4,3), (0,1,0,0,3), (0,3,1,0,2), (0,0,0,0,2), (0,1,1,0,2), (0,0,1,0,1), (0,0,1,1,2), (4,1), (0,2,0,1,3),
+    (0,2,1,1,2), (4,2), (0,3,1,1,2), (5,2), (5,1), (0,0,0,0,3), (0,0,1,0,2), (0,3,0,1,3), (4,0), (0,3,1,0,3),
+    (0,1,0,1,3), (0,2,1,0,2), (0,2,0,0,3), (0,3,1,1,3), (0,3,0,0,3), (5,3), (0,2,1,1,3), (0,1,1,1,2), (0,0,1,1,3),
+    (0,0,0,1,3), (6,3), (0,2,1,0,3), (6,2), (0,1,1,0,3), (5,0), (0,1,1,1,3), (7,3), (6,1), (7,2), (8,3), (0,0,1,0,3),
+    (7,1), (6,0), (8,2), (9,3), (8,1), (9,2), (7,0), (11,3), (10,2), (9,1), (13,3), (8,0), (11,2), (10,3), (9,0),
+    (15,3), (13,2), (10,1), (11,1), (16,3), (12,2), (13,1), (10,0), (11,0), (15,2), (14,2), (12,3), (13,0), (15,1),
+    (12,1), (12,0), (16,2), (14,3), (15,0), (17,2), (14,1), (16,1), (17,3), (14,0), (16,0), (17,1), (17,0),
 )
 
 
@@ -447,16 +448,23 @@
             done["tr", c][0].wait_send()
 
 
-def last(c_ref, ir_ref, iq_ref, out_ref):
-    tall, cols = out_ref.shape
+def last(c_ref, ir_ref, iq_ref, out_ref, total, sems):
+    rows, cols = total.shape
     block = pl.ds(al(lax.axis_index("k") * cols, cols), cols)
-    m = pl.ds(al(pl.program_id(0) * tall, tall), tall)
-    total = c_ref[m, :]
-    for p in range(2):
-        total += lax.dot_general(
-            ir_ref[p, m, :], iq_ref[p, block, :], (((1,), (1,)), ((), ())), preferred_element_type=F32
-        )
-    out_ref[...] = total
+    tall = rows // LAST
+    copies = []
+    for i in range(LAST):
+        m = pl.ds(i * tall, tall)
+        value = c_ref[m, :]
+        for p in range(2):
+            value += lax.dot_general(
+                ir_ref[p, m, :], iq_ref[p, block, :], (((1,), (1,)), ((), ())), preferred_element_type=F32
+            )
+        total[m, :] = value
+        copies.append(pltpu.make_async_copy(total.at[m], out_ref.at[m], sems.at[i]))
+        copies[-1].start()
+    for copy in copies:
+        copy.wait()
 
 
 def solution(mesh):
@@ -507,14 +515,13 @@
                 collective_id=0, has_side_effects=True, vmem_limit_bytes=50 * 1024 * 1024
             ),
         )(held, factor, inverses, covariance)
-        tall = 256
         return pl.pallas_call(
             last,
             out_shape=jax.ShapeDtypeStruct(covariance.shape, covariance.dtype),
-            grid=(rows // tall,),
             in_specs=[pl.BlockSpec(memory_space=pltpu.VMEM)] * 3,
-            out_specs=pl.BlockSpec((tall, cols), lambda i: (i, 0)),
-            compiler_params=pltpu.CompilerParams(vmem_limit_bytes=8 * 1024 * 1024),
+            out_specs=pl.BlockSpec(memory_space=pltpu.HBM),
+            scratch_shapes=[pltpu.VMEM((rows, cols), F32), pltpu.SemaphoreType.DMA((LAST,))],
+            compiler_params=pltpu.CompilerParams(vmem_limit_bytes=6 * 1024 * 1024),
         )(partial_sum, left, right)
 
     spec = P(("x", "zh"), ("zl", "y", "k"))

time: 118 us -> 113 us (0.958)
  Pallas kernels: 117 us -> 112 us
    pallas_call x1, Pallas kernels: 113 us -> 109 us  [body(): pl.pallas_call(kernel, out_shape=[pltpu.VMEM((rows, cols), F32), pltpu.VM...]
where the time goes in v5:
time: 113 us; the launch traced here: 112 us
  Pallas kernels  112 us (99%)
    pallas_call x1, Pallas kernels, body(): pl.pallas_call(kernel, out_shape=[pltpu.VMEM((rows, cols), F32), pltpu.VM...  109 us
    pallas_call x1, Pallas kernels, body(): pl.pallas_call(last, out_shape=jax.ShapeDtypeStruct(covariance.shape, cov...  3.16 us

profile of v5, /device:TPU:1, one launch (start us, length us, event | category | flops | bytes accessed | tf_op | source)
XLA Modules:
  0.0 111.9 jit_solution(3901443717282590224)
XLA Ops:
  0.0 108.7 %shard_map.46 = (f32[1536,768]{1,0:T(8,128)S(1)}, bf16[2,1536,256]{2,1,0:T(8,128)(2,1)S(1)}, bf16[2,1536,256]{2,1,0:T(8,128)(2,1)S(1)}) custom-call(bf16[1536,768]{1,0:T(8,128)(2,1)} %l_ref.1, bf16[2,768,128]{2,1,0:T(8,128)(2,1)} %f_ref.1, bf16[2,128,1024]{2,1,0:T(8,128)(2,1)} %d_ref.1, f32[1536,768]{1,0:T(8,128)} %c_ref.1), custom_call_target="tpu_custom_call" | custom-call | tf_op jit(solution)/shard_map/pallas_call | solution.py:481
  108.7 3.2 %shard_map.47 = f32[1536,768]{1,0:T(8,128)} custom-call(f32[1536,768]{1,0:T(8,128)S(1)} %get-tuple-element.8.c_ref, bf16[2,1536,256]{2,1,0:T(8,128)(2,1)S(1)} %get-tuple-element.9.ir_ref, bf16[2,1536,256]{2,1,0:T(8,128)(2,1)S(1)} %get-tuple-element.10.iq_ref), custom_call_target="tpu_custom_call" | custom-call | tf_op jit(solution)/shard_map/pallas_call | solution.py:518

commit v6 on v5

--- a/solution.py
+++ b/solution.py
@@ -356,9 +356,15 @@
         src = iqs[c].at[k, thin(got)]
         done["cgz", c] = remote(src, src, {"zh": 1 - zh})
 
+    def share(c, b):
+        src = irs[c].at[k, slab(b)]
+        done.setdefault(("ir", c), []).append(remote(src, src, {"k": 1 - k}))
+
     def s6a(c):
         for copy in done["agy", c]:
             copy.wait_recv()
+        for b in (y, yp, ym):
+            share(c, b)
         low, high = irs[c].at[k, thin(2 * ym)], irs[c].at[k, thin(2 * yp + 1)]
         done["agy2", c] = [remote(low, low, {"y": yp}), remote(high, high, {"y": ym})]
 
@@ -370,7 +376,7 @@
     def s7a(c):
         for copy in done["agy2", c]:
             copy.wait_recv()
-        done["ir", c] = remote(irs[c].at[k], irs[c].at[k], {"k": 1 - k})
+        share(c, y2)
 
     def s7b(c):
         for copy in done["cgx", c]:
@@ -385,7 +391,8 @@
         done["iq", c] = remote(src, src, {"k": 1 - k})
 
     def s9(c):
-        done["ir", c].wait_recv()
+        for copy in done["ir", c]:
+            copy.wait_recv()
         done["iq", c].wait_recv()
 
         @pl.loop(0, steps)
@@ -414,7 +421,8 @@
             if len(added) == CHUNKS:
                 break
         step(*args)
-    done["ir", final].wait_recv()
+    for copy in done["ir", final]:
+        copy.wait_recv()
     done["iq", final].wait_recv()
     for copy in sent + f_a:
         copy.wait_send()
@@ -477,7 +485,7 @@
         drows, width = inverses.shape[1:]
         wide = width // CHUNKS
         part = rows // 8
-        n_remote = 2 + 2 * SUB + 22 * CHUNKS
+        n_remote = 2 + 2 * SUB + 25 * CHUNKS
         partial_sum, left, right = pl.pallas_call(
             kernel,
             out_shape=[

time: 113 us -> 113 us (level)
  no operation moved by 1% of the time
where the time goes in v6:
time: 113 us; the launch traced here: 111 us
  Pallas kernels  111 us (98%)
    pallas_call x1, Pallas kernels, body(): pl.pallas_call(kernel, out_shape=[pltpu.VMEM((rows, cols), F32), pltpu.VM...  108 us
    pallas_call x1, Pallas kernels, body(): pl.pallas_call(last, out_shape=jax.ShapeDtypeStruct(covariance.shape, cov...  3.15 us

profile of v6, /device:TPU:1, one launch (start us, length us, event | category | flops | bytes accessed | tf_op | source)
XLA Modules:
  0.0 111.3 jit_solution(9142090220504127838)
XLA Ops:
  0.0 108.1 %shard_map.46 = (f32[1536,768]{1,0:T(8,128)S(1)}, bf16[2,1536,256]{2,1,0:T(8,128)(2,1)S(1)}, bf16[2,1536,256]{2,1,0:T(8,128)(2,1)S(1)}) custom-call(bf16[1536,768]{1,0:T(8,128)(2,1)} %l_ref.1, bf16[2,768,128]{2,1,0:T(8,128)(2,1)} %f_ref.1, bf16[2,128,1024]{2,1,0:T(8,128)(2,1)} %d_ref.1, f32[1536,768]{1,0:T(8,128)} %c_ref.1), custom_call_target="tpu_custom_call" | custom-call | tf_op jit(solution)/shard_map/pallas_call | solution.py:489
  108.1 3.2 %shard_map.47 = f32[1536,768]{1,0:T(8,128)} custom-call(f32[1536,768]{1,0:T(8,128)S(1)} %get-tuple-element.8.c_ref, bf16[2,1536,256]{2,1,0:T(8,128)(2,1)S(1)} %get-tuple-element.9.ir_ref, bf16[2,1536,256]{2,1,0:T(8,128)(2,1)S(1)} %get-tuple-element.10.iq_ref), custom_call_target="tpu_custom_call" | custom-call | tf_op jit(solution)/shard_map/pallas_call | solution.py:526
